TPU v7x, 32 devices: a whole 2x2x4 slice. The times are simulated.
32 devices in a mesh: dp: 4 (over y, x), ctx: 8 (over z, core).
Axes of the slice: x: 2, y: 2, z: 4, core: 2. Of those that a mesh axis runs over, the one named last changes fastest.
Arguments:
- block_input: float32 [4, 1024, 768], P('dp', 'ctx'), may hold values from -6 to 6
- out_cotangent: float32 [4, 1024, 768], P('dp', 'ctx'), may hold values from -6 to 6
- first_gain: float32 [768], replicated, may hold values from 0.25 to 1.75
- first_shift: float32 [768], replicated, may hold values from -3 to 3
- mix_weight: bfloat16 [768, 2304], P('dp'), may hold values from -0.21875 to 0.21875
- query_bias: float32 [768], replicated, may hold values from -3 to 3
- value_bias: float32 [768], replicated, may hold values from -3 to 3
- attn_weight: bfloat16 [768, 768], P('dp'), may hold values from -0.75 to 0.75
- attn_bias: float32 [768], replicated, may hold values from -3 to 3
- second_gain: float32 [768], replicated, may hold values from 0.25 to 1.75
- second_shift: float32 [768], replicated, may hold values from -3 to 3
- up_weight: bfloat16 [768, 3072], P('dp'), may hold values from -0.21875 to 0.21875
- up_bias: float32 [3072], replicated, may hold values from -3 to 3
- down_weight: bfloat16 [3072, 768], P('dp'), may hold values from -0.109375 to 0.109375
- down_bias: float32 [768], replicated, may hold values from -3 to 3
Outputs:
- block_output: float32 [4, 1024, 768], P('dp', 'ctx')
- input_grad: float32 [4, 1024, 768], P('dp', 'ctx')
- first_gain_grad: float32 [768], replicated
- first_shift_grad: float32 [768], replicated
- mix_weight_grad: float32 [768, 2304], P('dp')
- query_bias_grad: float32 [768], replicated
- value_bias_grad: float32 [768], replicated
- attn_weight_grad: float32 [768, 768], P('dp')
- attn_bias_grad: float32 [768], replicated
- second_gain_grad: float32 [768], replicated
- second_shift_grad: float32 [768], replicated
- up_weight_grad: float32 [768, 3072], P('dp')
- up_bias_grad: float32 [3072], replicated
- down_weight_grad: float32 [3072, 768], P('dp')
- down_bias_grad: float32 [768], replicated
All inputs are finite; a program needn't handle non-finite values.
Results may differ from a plain program's by a relative error of at most 0.023.
Values may be sent and summed in bfloat16 or wider, within the bound.
A program may use at most 128 MiB of HBM per device.

v0:
```python
import math
import jax
import jax.numpy as jnp
from jax import lax
from jax.sharding import PartitionSpec as P

H = 12
HD = 64
EPS = 1e-05
GELU_C = math.sqrt(2.0 / math.pi)


def from_behind(value, axis, steps):
    count = lax.axis_size(axis)
    pairs = [(source, (source + steps) % count) for source in range(count)]
    return lax.ppermute(value, axis, pairs)


def layer_norm(x, gain, shift):
    centered = x - jnp.mean(x, axis=-1, keepdims=True)
    rstd = lax.rsqrt(jnp.mean(centered * centered, axis=-1, keepdims=True) + EPS)
    x_hat = centered * rstd
    return (x_hat, rstd, x_hat * gain + shift)


def norm_back(grad, x_hat, rstd, gain):
    g = grad * gain
    return rstd * (
        g
        - jnp.mean(g, axis=-1, keepdims=True)
        - x_hat * jnp.mean(g * x_hat, axis=-1, keepdims=True)
    )


def gelu_pair(u):
    inner = GELU_C * (u + 0.044715 * u * u * u)
    t = jnp.tanh(inner)
    value = 0.5 * u * (1.0 + t)
    slope = 0.5 * (1.0 + t) + 0.5 * u * (1.0 - t * t) * GELU_C * (1.0 + 3.0 * 0.044715 * u * u)
    return (value, slope)


def matmul(a, b):
    return jnp.dot(a, b, preferred_element_type=jnp.float32)


def matmul_tn(a, b):
    return lax.dot_general(a, b, (((0,), (0,)), ((), ())), preferred_element_type=jnp.float32)


def matmul_nt(a, b):
    return lax.dot_general(a, b, (((1,), (1,)), ((), ())), preferred_element_type=jnp.float32)


def body(
    block_input,
    out_cotangent,
    first_gain,
    first_shift,
    mix_weight,
    query_bias,
    value_bias,
    attn_weight,
    attn_bias,
    second_gain,
    second_shift,
    up_weight,
    up_bias,
    down_weight,
    down_bias,
):
    rows = block_input.shape[1]
    width = block_input.shape[2]
    scale = HD ** (-0.5)
    x_rows = block_input.reshape(rows, width)
    cot = out_cotangent.reshape(rows, width)
    mix_full, attn_full, up_full, down_full = (
        lax.all_gather(mix_weight, "dp", axis=0, tiled=True),
        lax.all_gather(attn_weight, "dp", axis=0, tiled=True),
        lax.all_gather(up_weight, "dp", axis=0, tiled=True),
        lax.all_gather(down_weight, "dp", axis=0, tiled=True),
    )
    first_hat, first_rstd, first_out = layer_norm(x_rows, first_gain, first_shift)
    first_in = first_out.astype(jnp.bfloat16)
    mixed = matmul(first_in, mix_full)
    queries = (mixed[:, :width] + query_bias).astype(jnp.bfloat16)
    keys = mixed[:, width : 2 * width].astype(jnp.bfloat16)
    values = (mixed[:, 2 * width :] + value_bias).astype(jnp.bfloat16)
    q3 = queries.reshape(rows, H, HD)
    me = lax.axis_index("ctx")
    cycle_size = lax.axis_size("ctx")
    q_pos = me * rows + jnp.arange(rows)
    q_last = me * rows + rows - 1
    start_state = (
        jnp.full((H, rows), -1e30, jnp.float32),
        jnp.zeros((H, rows), jnp.float32),
        jnp.zeros((H, rows, HD), jnp.float32),
    )
    carry = start_state
    key_piece = lax.all_gather(keys, "ctx", axis=0, tiled=True)
    value_piece = lax.all_gather(values, "ctx", axis=0, tiled=True)
    count = key_piece.shape[0]
    kblock = math.gcd(count, 512)
    nblocks = count // kblock
    key_blocks = key_piece.reshape(nblocks, kblock, H, HD)
    value_blocks = value_piece.reshape(nblocks, kblock, H, HD)
    offsets = jnp.arange(nblocks) * kblock

    def one_block(state, item):
        key_blk, value_blk, offset = item

        def compute(state_in):
            run_max, run_total, run_acc = state_in
            key_pos = offset + jnp.arange(kblock)
            allowed = (key_pos[None, :] <= q_pos[:, None])[None]
            scores = (
                jnp.einsum("qhd,khd->hqk", q3, key_blk, preferred_element_type=jnp.float32) * scale
            )
            scores = jnp.where(allowed, scores, -1e30)
            new_max = jnp.maximum(run_max, jnp.max(scores, axis=-1))
            expo = jnp.where(allowed, jnp.exp(scores - new_max[..., None]), 0.0)
            factor = jnp.exp(run_max - new_max)
            new_total = run_total * factor + jnp.sum(expo, axis=-1)
            new_acc = run_acc * factor[..., None] + jnp.einsum(
                "hqk,khd->hqd", expo, value_blk.astype(jnp.float32), precision=lax.Precision.HIGHEST
            )
            return (new_max, new_total, new_acc)

        def keep_state(state_in):
            return state_in

        return (lax.cond(offset <= q_last, compute, keep_state, state), None)

    carry, unused = lax.scan(one_block, carry, (key_blocks, value_blocks, offsets))
    run_max, run_total, run_acc = carry
    attended = (
        (run_acc / run_total[..., None])
        .transpose(1, 0, 2)
        .reshape(rows, width)
        .astype(jnp.bfloat16)
    )
    lse = run_max + jnp.log(run_total)
    after_attn = x_rows + matmul(attended, attn_full) + attn_bias
    second_hat, second_rstd, second_out = layer_norm(after_attn, second_gain, second_shift)
    second_in = second_out.astype(jnp.bfloat16)
    pre_act = matmul(second_in, up_full) + up_bias
    act_value, act_slope = gelu_pair(pre_act)
    activ = act_value.astype(jnp.bfloat16)
    block_output = after_attn + matmul(activ, down_full) + down_bias
    mix_back, attn_back, up_back, down_back = (
        lax.all_gather(mix_weight, "dp", axis=0, tiled=True),
        lax.all_gather(attn_weight, "dp", axis=0, tiled=True),
        lax.all_gather(up_weight, "dp", axis=0, tiled=True),
        lax.all_gather(down_weight, "dp", axis=0, tiled=True),
    )
    cot_b = cot.astype(jnp.bfloat16)
    down_weight_grad = matmul_tn(activ, cot_b)
    down_bias_grad = jnp.sum(cot, axis=0)
    pre_grad = matmul_nt(cot_b, down_back) * act_slope
    pre_grad_b = pre_grad.astype(jnp.bfloat16)
    up_weight_grad = matmul_tn(second_in, pre_grad_b)
    up_bias_grad = jnp.sum(pre_grad, axis=0)
    second_grad = matmul_nt(pre_grad_b, up_back)
    second_gain_grad = jnp.sum(second_grad * second_hat, axis=0)
    second_shift_grad = jnp.sum(second_grad, axis=0)
    resid_grad = cot + norm_back(second_grad, second_hat, second_rstd, second_gain)
    resid_b = resid_grad.astype(jnp.bfloat16)
    attn_weight_grad = matmul_tn(attended, resid_b)
    attn_bias_grad = jnp.sum(resid_grad, axis=0)
    attended_grad = matmul_nt(resid_b, attn_back).astype(jnp.bfloat16)
    grad3 = attended_grad.reshape(rows, H, HD)
    delta = jnp.sum(
        grad3.astype(jnp.float32) * attended.astype(jnp.float32).reshape(rows, H, HD), axis=-1
    ).T

    def block_grads(key_blk, value_blk, key_start):
        count = key_blk.shape[0]
        key3 = key_blk.reshape(count, H, HD)
        value3 = value_blk.reshape(count, H, HD)
        key_pos = key_start + jnp.arange(count)
        allowed = (key_pos[None, :] <= q_pos[:, None])[None]
        scores = jnp.einsum("qhd,khd->hqk", q3, key3, preferred_element_type=jnp.float32) * scale
        probs = jnp.where(allowed, jnp.exp(scores - lse[..., None]), 0.0)
        dprob = jnp.einsum("qhd,khd->hqk", grad3, value3, preferred_element_type=jnp.float32)
        dscore = probs * (dprob - delta[..., None])
        probs_b = probs.astype(jnp.bfloat16)
        dscore_b = dscore.astype(jnp.bfloat16)
        value_add = jnp.einsum("hqk,qhd->khd", probs_b, grad3, preferred_element_type=jnp.float32)
        key_add = (
            jnp.einsum("hqk,qhd->khd", dscore_b, q3, preferred_element_type=jnp.float32) * scale
        )
        query_add = (
            jnp.einsum("hqk,khd->qhd", dscore_b, key3, preferred_element_type=jnp.float32) * scale
        )
        return (
            query_add.reshape(rows, width),
            key_add.reshape(count, width),
            value_add.reshape(count, width),
        )

    def skip_grads(key_blk, value_blk, key_start):
        count = key_blk.shape[0]
        empty = jnp.zeros((count, width), jnp.float32)
        return (jnp.zeros((rows, width), jnp.float32), empty, empty)

    zeros = jnp.zeros((rows, width), jnp.float32)

    def pass_grads(key_acc, value_acc):
        return (
            from_behind(key_acc.astype(jnp.bfloat16), "ctx", -1).astype(key_acc.dtype),
            from_behind(value_acc.astype(jnp.bfloat16), "ctx", -1).astype(value_acc.dtype),
        )

    def cycle_turn(step, state):
        key_blk, value_blk, key_acc, value_acc, query_acc = state
        owner = (me + step) % cycle_size
        query_add, key_add, value_add = lax.cond(
            owner <= me, block_grads, skip_grads, key_blk, value_blk, owner * rows
        )
        key_blk, value_blk = from_behind((key_blk, value_blk), "ctx", -1)
        key_acc, value_acc = pass_grads(key_acc + key_add, value_acc + value_add)
        return (key_blk, value_blk, key_acc, value_acc, query_acc + query_add)

    key_blk, value_blk, key_acc, value_acc, query_acc = lax.fori_loop(
        0, cycle_size - 1, cycle_turn, (keys, values, zeros, zeros, zeros)
    )
    last_owner = (me + cycle_size - 1) % cycle_size
    query_add, key_add, value_add = lax.cond(
        last_owner <= me, block_grads, skip_grads, key_blk, value_blk, last_owner * rows
    )
    key_grad, value_grad = pass_grads(key_acc + key_add, value_acc + value_add)
    query_grad = query_acc + query_add
    query_bias_grad = jnp.sum(query_grad, axis=0)
    value_bias_grad = jnp.sum(value_grad, axis=0)
    mixed_grad = jnp.concatenate([query_grad, key_grad, value_grad], axis=1).astype(jnp.bfloat16)
    mix_weight_grad = matmul_tn(first_in, mixed_grad)
    first_grad = matmul_nt(mixed_grad, mix_back)
    first_gain_grad = jnp.sum(first_grad * first_hat, axis=0)
    first_shift_grad = jnp.sum(first_grad, axis=0)
    input_grad = resid_grad + norm_back(first_grad, first_hat, first_rstd, first_gain)
    local_mats = (mix_weight_grad, attn_weight_grad, up_weight_grad, down_weight_grad)
    shard_sums = (
        lax.psum_scatter(
            local_mats[0].astype(jnp.bfloat16), "dp", scatter_dimension=0, tiled=True
        ).astype(jnp.float32),
        lax.psum_scatter(
            local_mats[1].astype(jnp.bfloat16), "dp", scatter_dimension=0, tiled=True
        ).astype(jnp.float32),
        lax.psum_scatter(
            local_mats[2].astype(jnp.bfloat16), "dp", scatter_dimension=0, tiled=True
        ).astype(jnp.float32),
        lax.psum_scatter(
            local_mats[3].astype(jnp.bfloat16), "dp", scatter_dimension=0, tiled=True
        ).astype(jnp.float32),
    )
    mats = (
        lax.psum(shard_sums[0].astype(jnp.bfloat16), "ctx").astype(jnp.float32),
        lax.psum(shard_sums[1].astype(jnp.bfloat16), "ctx").astype(jnp.float32),
        lax.psum(shard_sums[2].astype(jnp.bfloat16), "ctx").astype(jnp.float32),
        lax.psum(shard_sums[3].astype(jnp.bfloat16), "ctx").astype(jnp.float32),
    )
    smalls = lax.psum(
        (
            first_gain_grad,
            first_shift_grad,
            query_bias_grad,
            value_bias_grad,
            attn_bias_grad,
            second_gain_grad,
            second_shift_grad,
            up_bias_grad,
            down_bias_grad,
        ),
        ("dp", "ctx"),
    )
    return (
        block_output.reshape(1, rows, width),
        input_grad.reshape(1, rows, width),
        smalls[0],
        smalls[1],
        mats[0],
        smalls[2],
        smalls[3],
        mats[1],
        smalls[4],
        smalls[5],
        smalls[6],
        mats[2],
        smalls[7],
        mats[3],
        smalls[8],
    )


def solution(mesh):
    placed = (
        P("dp", "ctx", None),
        P("dp", "ctx", None),
        P(),
        P(),
        P("dp", None),
        P(),
        P(),
        P("dp", None),
        P(),
        P(),
        P(),
        P("dp", None),
        P(),
        P("dp", None),
        P(),
    )
    return jax.shard_map(
        body,
        mesh=mesh,
        in_specs=placed,
        out_specs=(
            P("dp", "ctx", None),
            P("dp", "ctx", None),
            P(),
            P(),
            P("dp", None),
            P(),
            P(),
            P("dp", None),
            P(),
            P(),
            P(),
            P("dp", None),
            P(),
            P("dp", None),
            P(),
        ),
        check_vma=False,
    )
```

profile of v0, /device:TPU:0, one launch (start us, length us, event | category | flops | bytes accessed | tf_op | source)
XLA Modules:
  0.0 692.6 jit_solution(13095653264918594262)
XLA Ops:
  10.4 49.4 %all-gather.7.cloned.1.call-done = bf16[768,2304]{1,0:T(8,128)(2,1)} async-done(((bf16[192,2304]{1,0:T(8,128)(2,1)}), bf16[768,2304]{1,0:T(8,128)(2,1)}) %all-gather.7.cloned.1.call-update) | async-done | bytes 3538960 | tf_op jit(solution)/shard_map/all_gather | solution.py:78
  67.7 20.9 %all-gather.9.cloned.1.call-done = bf16[1024,768]{1,0:T(8,128)(2,1)} async-done(((bf16[128,768]{1,0:T(8,128)(2,1)}), bf16[1024,768]{1,0:T(8,128)(2,1)}) %all-gather.9.cloned.1.call-update) | async-done | bytes 1572880 | tf_op jit(solution)/shard_map/all_gather | solution.py:100
  94.4 20.8 %all-gather.11.cloned.1.call-done = bf16[1024,768]{1,0:T(8,128)(2,1)} async-done(((bf16[128,768]{1,0:T(8,128)(2,1)}), bf16[1024,768]{1,0:T(8,128)(2,1)}) %all-gather.11.cloned.1.call-update) | async-done | bytes 1572880 | tf_op jit(solution)/shard_map/all_gather | solution.py:101
  117.8 3.8 reshape.243
  125.4 8.6 %while.39 = (s32[]{:T(128)}, f32[12,128]{1,0:T(8,128)S(1)}, f32[12,128]{1,0:T(8,128)S(1)}, f32[12,128,64]{1,2,0:T(8,128)}, s32[2]{0:T(128)S(1)}, /*index=5*/s32[...) while((s32[]{:T(128)}, f32[12,128]{1,0:T(8,128)S(1)}, ...), condition=%wide.region_7.8_spmd.clone, body=%wide.region_2.7_spmd.clone.sunk | while | flops 714346112 | bytes 21801340 | solution.py:134
  126.6 6.1 conditional.8
  135.1 8.6 %all-gather.13.cloned.1.call-done = bf16[768,768]{1,0:T(8,128)(2,1)} async-done(((bf16[192,768]{1,0:T(8,128)(2,1)}), bf16[768,768]{1,0:T(8,128)(2,1)}) %all-gather.13.cloned.1.call-update) | async-done | bytes 1179664 | tf_op jit(solution)/shard_map/all_gather | solution.py:79
  146.2 56.1 %all-gather.15.cloned.1.call-done = bf16[768,3072]{1,0:T(8,128)(2,1)} async-done(((bf16[192,3072]{1,0:T(8,128)(2,1)}), bf16[768,3072]{1,0:T(8,128)(2,1)}) %all-gather.15.cloned.1.call-update) | async-done | bytes 4718608 | tf_op jit(solution)/shard_map/all_gather | solution.py:80
  202.4 4.3 convolution_add_fusion
  206.7 54.3 %all-gather.17.cloned.1.call-done = bf16[3072,768]{1,0:T(8,128)(2,1)} async-done(((bf16[768,768]{1,0:T(8,128)(2,1)}), bf16[3072,768]{1,0:T(8,128)(2,1)}) %all-gather.17.cloned.1.call-update) | async-done | bytes 4718608 | tf_op jit(solution)/shard_map/all_gather | solution.py:81
  261.0 5.4 fusion.63
  273.4 132.6 %while.40 = (s32[]{:T(128)}, bf16[128,768]{0,1:T(8,128)(2,1)}, bf16[128,768]{0,1:T(8,128)(2,1)}, f32[128,768]{0,1:T(8,128)S(1)}, f32[128,768]{0,1:T(8,128)S(1)},...) while((s32[]{:T(128)}, bf16[128,768]{0,1:T(8,128)(2,1)}, ...), condition=%wide.region_16.17_spmd.clone, body=%wide.region_13.16_spmd.clone.sunk | while | flops 128401680 | bytes 14401084 | solution.py:224
  280.6 5.2 conditional.9
  300.4 5.1 collective-permute-start.2
  312.7 3.7 collective-permute-start
  319.4 5.1 collective-permute-start.2
  331.7 3.7 collective-permute-start
  338.4 5.1 collective-permute-start.2
  350.7 3.7 collective-permute-start
  357.3 5.1 collective-permute-start.2
  369.6 3.7 collective-permute-start
  376.3 5.1 collective-permute-start.2
  388.6 3.7 collective-permute-start
  395.3 5.1 collective-permute-start.2
  406.6 8.9 %collective-permute-start.5 = (bf16[128,768]{0,1:T(8,128)(2,1)S(1)}, bf16[128,768]{0,1:T(8,128)(2,1)S(1)}, u32[]{:S(2)}, u32[]{:S(2)}) collective-permute-start(bf16[128,768]{0,1:T(8,128)(2,1)S(1)} %add_convert_fusion), channel_id=1, source_target_pairs={{0,7},{1,0},{2,1},{3,2},{4,3},{5,4},{6,5},{7,6},{8,15},{9,8},{10,9... | collective-permute-start | bytes 589832 | tf_op jit(solution)/shard_map/ppermute | solution.py:16
  429.7 5.4 convolution_convert_fusion
  435.1 36.4 %reduce-scatter.5.cloned.1.call-done = bf16[192,2304]{1,0:T(8,128)(2,1)} async-done(((bf16[768,2304]{1,0:T(8,128)(2,1)}), bf16[192,2304]{1,0:T(8,128)(2,1)}) %reduce-scatter.5.cloned.1.call-update) | async-done | bytes 884752 | tf_op jit(solution)/shard_map/reduce_scatter | solution.py:243
  471.6 60.0 %reduce-scatter.9.cloned.1.call-done = bf16[192,3072]{1,0:T(8,128)(2,1)} async-done(((bf16[768,3072]{1,0:T(8,128)(2,1)}), bf16[192,3072]{1,0:T(8,128)(2,1)}) %reduce-scatter.9.cloned.1.call-update) | async-done | bytes 1179664 | tf_op jit(solution)/shard_map/reduce_scatter | solution.py:249
  531.6 59.8 %reduce-scatter.11.cloned.1.call-done = bf16[768,768]{1,0:T(8,128)(2,1)} async-done(((bf16[3072,768]{1,0:T(8,128)(2,1)}), bf16[768,768]{1,0:T(8,128)(2,1)}) %reduce-scatter.11.cloned.1.call-update) | async-done | bytes 1179664 | tf_op jit(solution)/shard_map/reduce_scatter | solution.py:252
  592.1 4.8 fusion.46
  598.6 42.0 %all-reduce = (f32[768]{0:T(1024)}, f32[768]{0:T(1024)}, f32[768]{0:T(1024)}, f32[768]{0:T(1024)}, f32[768]{0:T(1024)}, /*index=5*/f32[768]{0:T(1024)}, f32[768]{0:T(1024)}, f32[3072]{0:T(1024)}, f32[768]{0:T(1024)}) all-reduce(f32[768]{0:T(1024)S(1)} %get-tuple-element.662, ...), channel_id=1, replica_groups=mesh['dp'=4,'ctx'=8] {'dp','ctx'}, use_global_device_ids=true, to_apply=%region_22.23 | all-reduce | flops 9216 | bytes 73728 | tf_op jit(solution)/shard_map/psum | solution.py:262
  641.5 37.8 %all-reduce.4.cloned.1.call-done = (bf16[192,2304]{1,0:T(8,128)(2,1)}, bf16[192,768]{1,0:T(8,128)(2,1)}, bf16[192,3072]{1,0:T(8,128)(2,1)}, bf16[768,768]{1,0:T(8,128)(2,1)}) async-done(((bf16[192,2304]{1,0:T(8,128)(2,1)}, bf16[192,768]{1,0:T(8,128)(2,1)}, bf16[192,3072]{1,0:T(8,128)(2,1)}, bf16[768,768]{1,0:T(8,128)(2,1)}), (bf16[192,2304]{1,0:T(8,128)(2,1)}, bf16[192,768]{1,0:T(8,128)(2,1)}, ...) | async-done | bytes 3538960 | tf_op jit(solution)/shard_map/psum | solution.py:257
  (313 shorter events, 148.9 us)
Async XLA Ops:
  7.2 52.5 %all-gather.7.cloned.1.call-start = ((), (), s32[]{:S(2)}) async-start(), calls=%async_computation.4 | async-start | bytes 4423680 | tf_op jit(solution)/shard_map/all_gather | solution.py:78
  7.9 80.7 %all-gather.9.cloned.1.call-start = ((), (), s32[]{:S(2)}) async-start(), calls=%async_computation.5 | async-start | bytes 1769472 | tf_op jit(solution)/shard_map/all_gather | solution.py:100
  63.2 52.1 %all-gather.11.cloned.1.call-start = ((), (), s32[]{:S(2)}) async-start(), calls=%async_computation.6 | async-start | bytes 1769472 | tf_op jit(solution)/shard_map/all_gather | solution.py:101
  64.0 79.7 %all-gather.13.cloned.1.call-start = ((), (), s32[]{:S(2)}) async-start(), calls=%async_computation.7 | async-start | bytes 1474560 | tf_op jit(solution)/shard_map/all_gather | solution.py:79
  64.6 137.7 %all-gather.15.cloned.1.call-start = ((), (), s32[]{:S(2)}) async-start(), calls=%async_computation.8 | async-start | bytes 5898240 | tf_op jit(solution)/shard_map/all_gather | solution.py:80
  65.2 195.8 %all-gather.17.cloned.1.call-start = ((), (), s32[]{:S(2)}) async-start(), calls=%async_computation.9 | async-start | bytes 5898240 | tf_op jit(solution)/shard_map/all_gather | solution.py:81
  65.8 369.4 %reduce-scatter.7.cloned.1.call-start = ((), (), s32[]{:S(2)}) async-start(), calls=%async_computation.11 | async-start | bytes 1474560 | tf_op jit(solution)/shard_map/reduce_scatter | solution.py:246
  273.1 198.4 %reduce-scatter.5.cloned.1.call-start = ((), (), s32[]{:S(2)}) async-start(), calls=%async_computation.10 | async-start | bytes 4423680 | tf_op jit(solution)/shard_map/reduce_scatter | solution.py:243
  275.0 17.1 %collective-permute-start = (bf16[128,768]{0,1:T(8,128)(2,1)}, bf16[128,768]{0,1:T(8,128)(2,1)}, u32[]{:S(2)}, u32[]{:S(2)}) collective-permute-start(bf16[128,768]{0,1:T(8,128)(2,1)} %copy.82), channel_id=1, source_target_pairs={{0,7},{1,0},{2,1},{3,2},{4,3},{5,4},{6,5},{7,6},{8,15},{9,8},{10,9... | collective-permute-start | bytes 589832 | tf_op jit(solution)/shard_map/while/body/eval_jaxpr/ppermute | solution.py:16
  279.2 12.9 %collective-permute-start.1 = (bf16[128,768]{0,1:T(8,128)(2,1)}, bf16[128,768]{0,1:T(8,128)(2,1)}, u32[]{:S(2)}, u32[]{:S(2)}) collective-permute-start(bf16[128,768]{0,1:T(8,128)(2,1)} %copy.83), channel_id=1, source_target_pairs={{0,7},{1,0},{2,1},{3,2},{4,3},{5,4},{6,5},{7,6},{8,15},{9,8},{10,9... | collective-permute-start | bytes 589832 | tf_op jit(solution)/shard_map/while/body/eval_jaxpr/ppermute | solution.py:16
  293.8 17.3 %collective-permute-start = (bf16[128,768]{0,1:T(8,128)(2,1)}, bf16[128,768]{0,1:T(8,128)(2,1)}, u32[]{:S(2)}, u32[]{:S(2)}) collective-permute-start(bf16[128,768]{0,1:T(8,128)(2,1)} %copy.82), channel_id=1, source_target_pairs={{0,7},{1,0},{2,1},{3,2},{4,3},{5,4},{6,5},{7,6},{8,15},{9,8},{10,9... | collective-permute-start | bytes 589832 | tf_op jit(solution)/shard_map/while/body/eval_jaxpr/ppermute | solution.py:16
  299.1 12.0 %collective-permute-start.1 = (bf16[128,768]{0,1:T(8,128)(2,1)}, bf16[128,768]{0,1:T(8,128)(2,1)}, u32[]{:S(2)}, u32[]{:S(2)}) collective-permute-start(bf16[128,768]{0,1:T(8,128)(2,1)} %copy.83), channel_id=1, source_target_pairs={{0,7},{1,0},{2,1},{3,2},{4,3},{5,4},{6,5},{7,6},{8,15},{9,8},{10,9... | collective-permute-start | bytes 589832 | tf_op jit(solution)/shard_map/while/body/eval_jaxpr/ppermute | solution.py:16
  300.4 8.6 %collective-permute-start.2 = (bf16[128,768]{0,1:T(8,128)(2,1)}, bf16[128,768]{0,1:T(8,128)(2,1)S(1)}, u32[]{:S(2)}, u32[]{:S(2)}) collective-permute-start(bf16[128,768]{0,1:T(8,128)(2,1)} %fusion.105), channel_id=1, source_target_pairs={{0,7},{1,0},{2,1},{3,2},{4,3},{5,4},{6,5},{7,6},{8,15},{9,8},{10,9... | collective-permute-start | bytes 589832 | tf_op jit(solution)/shard_map/while/body/eval_jaxpr/ppermute | solution.py:16
  312.7 17.3 %collective-permute-start = (bf16[128,768]{0,1:T(8,128)(2,1)}, bf16[128,768]{0,1:T(8,128)(2,1)}, u32[]{:S(2)}, u32[]{:S(2)}) collective-permute-start(bf16[128,768]{0,1:T(8,128)(2,1)} %copy.82), channel_id=1, source_target_pairs={{0,7},{1,0},{2,1},{3,2},{4,3},{5,4},{6,5},{7,6},{8,15},{9,8},{10,9... | collective-permute-start | bytes 589832 | tf_op jit(solution)/shard_map/while/body/eval_jaxpr/ppermute | solution.py:16
  318.0 12.0 %collective-permute-start.1 = (bf16[128,768]{0,1:T(8,128)(2,1)}, bf16[128,768]{0,1:T(8,128)(2,1)}, u32[]{:S(2)}, u32[]{:S(2)}) collective-permute-start(bf16[128,768]{0,1:T(8,128)(2,1)} %copy.83), channel_id=1, source_target_pairs={{0,7},{1,0},{2,1},{3,2},{4,3},{5,4},{6,5},{7,6},{8,15},{9,8},{10,9... | collective-permute-start | bytes 589832 | tf_op jit(solution)/shard_map/while/body/eval_jaxpr/ppermute | solution.py:16
  319.4 8.6 %collective-permute-start.2 = (bf16[128,768]{0,1:T(8,128)(2,1)}, bf16[128,768]{0,1:T(8,128)(2,1)S(1)}, u32[]{:S(2)}, u32[]{:S(2)}) collective-permute-start(bf16[128,768]{0,1:T(8,128)(2,1)} %fusion.105), channel_id=1, source_target_pairs={{0,7},{1,0},{2,1},{3,2},{4,3},{5,4},{6,5},{7,6},{8,15},{9,8},{10,9... | collective-permute-start | bytes 589832 | tf_op jit(solution)/shard_map/while/body/eval_jaxpr/ppermute | solution.py:16
  331.7 17.3 %collective-permute-start = (bf16[128,768]{0,1:T(8,128)(2,1)}, bf16[128,768]{0,1:T(8,128)(2,1)}, u32[]{:S(2)}, u32[]{:S(2)}) collective-permute-start(bf16[128,768]{0,1:T(8,128)(2,1)} %copy.82), channel_id=1, source_target_pairs={{0,7},{1,0},{2,1},{3,2},{4,3},{5,4},{6,5},{7,6},{8,15},{9,8},{10,9... | collective-permute-start | bytes 589832 | tf_op jit(solution)/shard_map/while/body/eval_jaxpr/ppermute | solution.py:16
  337.0 12.0 %collective-permute-start.1 = (bf16[128,768]{0,1:T(8,128)(2,1)}, bf16[128,768]{0,1:T(8,128)(2,1)}, u32[]{:S(2)}, u32[]{:S(2)}) collective-permute-start(bf16[128,768]{0,1:T(8,128)(2,1)} %copy.83), channel_id=1, source_target_pairs={{0,7},{1,0},{2,1},{3,2},{4,3},{5,4},{6,5},{7,6},{8,15},{9,8},{10,9... | collective-permute-start | bytes 589832 | tf_op jit(solution)/shard_map/while/body/eval_jaxpr/ppermute | solution.py:16
  338.4 8.6 %collective-permute-start.2 = (bf16[128,768]{0,1:T(8,128)(2,1)}, bf16[128,768]{0,1:T(8,128)(2,1)S(1)}, u32[]{:S(2)}, u32[]{:S(2)}) collective-permute-start(bf16[128,768]{0,1:T(8,128)(2,1)} %fusion.105), channel_id=1, source_target_pairs={{0,7},{1,0},{2,1},{3,2},{4,3},{5,4},{6,5},{7,6},{8,15},{9,8},{10,9... | collective-permute-start | bytes 589832 | tf_op jit(solution)/shard_map/while/body/eval_jaxpr/ppermute | solution.py:16
  350.7 17.3 %collective-permute-start = (bf16[128,768]{0,1:T(8,128)(2,1)}, bf16[128,768]{0,1:T(8,128)(2,1)}, u32[]{:S(2)}, u32[]{:S(2)}) collective-permute-start(bf16[128,768]{0,1:T(8,128)(2,1)} %copy.82), channel_id=1, source_target_pairs={{0,7},{1,0},{2,1},{3,2},{4,3},{5,4},{6,5},{7,6},{8,15},{9,8},{10,9... | collective-permute-start | bytes 589832 | tf_op jit(solution)/shard_map/while/body/eval_jaxpr/ppermute | solution.py:16
  356.0 12.0 %collective-permute-start.1 = (bf16[128,768]{0,1:T(8,128)(2,1)}, bf16[128,768]{0,1:T(8,128)(2,1)}, u32[]{:S(2)}, u32[]{:S(2)}) collective-permute-start(bf16[128,768]{0,1:T(8,128)(2,1)} %copy.83), channel_id=1, source_target_pairs={{0,7},{1,0},{2,1},{3,2},{4,3},{5,4},{6,5},{7,6},{8,15},{9,8},{10,9... | collective-permute-start | bytes 589832 | tf_op jit(solution)/shard_map/while/body/eval_jaxpr/ppermute | solution.py:16
  357.3 8.6 %collective-permute-start.2 = (bf16[128,768]{0,1:T(8,128)(2,1)}, bf16[128,768]{0,1:T(8,128)(2,1)S(1)}, u32[]{:S(2)}, u32[]{:S(2)}) collective-permute-start(bf16[128,768]{0,1:T(8,128)(2,1)} %fusion.105), channel_id=1, source_target_pairs={{0,7},{1,0},{2,1},{3,2},{4,3},{5,4},{6,5},{7,6},{8,15},{9,8},{10,9... | collective-permute-start | bytes 589832 | tf_op jit(solution)/shard_map/while/body/eval_jaxpr/ppermute | solution.py:16
  369.6 17.3 %collective-permute-start = (bf16[128,768]{0,1:T(8,128)(2,1)}, bf16[128,768]{0,1:T(8,128)(2,1)}, u32[]{:S(2)}, u32[]{:S(2)}) collective-permute-start(bf16[128,768]{0,1:T(8,128)(2,1)} %copy.82), channel_id=1, source_target_pairs={{0,7},{1,0},{2,1},{3,2},{4,3},{5,4},{6,5},{7,6},{8,15},{9,8},{10,9... | collective-permute-start | bytes 589832 | tf_op jit(solution)/shard_map/while/body/eval_jaxpr/ppermute | solution.py:16
  374.9 12.0 %collective-permute-start.1 = (bf16[128,768]{0,1:T(8,128)(2,1)}, bf16[128,768]{0,1:T(8,128)(2,1)}, u32[]{:S(2)}, u32[]{:S(2)}) collective-permute-start(bf16[128,768]{0,1:T(8,128)(2,1)} %copy.83), channel_id=1, source_target_pairs={{0,7},{1,0},{2,1},{3,2},{4,3},{5,4},{6,5},{7,6},{8,15},{9,8},{10,9... | collective-permute-start | bytes 589832 | tf_op jit(solution)/shard_map/while/body/eval_jaxpr/ppermute | solution.py:16
  376.3 8.6 %collective-permute-start.2 = (bf16[128,768]{0,1:T(8,128)(2,1)}, bf16[128,768]{0,1:T(8,128)(2,1)S(1)}, u32[]{:S(2)}, u32[]{:S(2)}) collective-permute-start(bf16[128,768]{0,1:T(8,128)(2,1)} %fusion.105), channel_id=1, source_target_pairs={{0,7},{1,0},{2,1},{3,2},{4,3},{5,4},{6,5},{7,6},{8,15},{9,8},{10,9... | collective-permute-start | bytes 589832 | tf_op jit(solution)/shard_map/while/body/eval_jaxpr/ppermute | solution.py:16
  388.6 17.3 %collective-permute-start = (bf16[128,768]{0,1:T(8,128)(2,1)}, bf16[128,768]{0,1:T(8,128)(2,1)}, u32[]{:S(2)}, u32[]{:S(2)}) collective-permute-start(bf16[128,768]{0,1:T(8,128)(2,1)} %copy.82), channel_id=1, source_target_pairs={{0,7},{1,0},{2,1},{3,2},{4,3},{5,4},{6,5},{7,6},{8,15},{9,8},{10,9... | collective-permute-start | bytes 589832 | tf_op jit(solution)/shard_map/while/body/eval_jaxpr/ppermute | solution.py:16
  393.9 12.0 %collective-permute-start.1 = (bf16[128,768]{0,1:T(8,128)(2,1)}, bf16[128,768]{0,1:T(8,128)(2,1)}, u32[]{:S(2)}, u32[]{:S(2)}) collective-permute-start(bf16[128,768]{0,1:T(8,128)(2,1)} %copy.83), channel_id=1, source_target_pairs={{0,7},{1,0},{2,1},{3,2},{4,3},{5,4},{6,5},{7,6},{8,15},{9,8},{10,9... | collective-permute-start | bytes 589832 | tf_op jit(solution)/shard_map/while/body/eval_jaxpr/ppermute | solution.py:16
  395.3 8.6 %collective-permute-start.2 = (bf16[128,768]{0,1:T(8,128)(2,1)}, bf16[128,768]{0,1:T(8,128)(2,1)S(1)}, u32[]{:S(2)}, u32[]{:S(2)}) collective-permute-start(bf16[128,768]{0,1:T(8,128)(2,1)} %fusion.105), channel_id=1, source_target_pairs={{0,7},{1,0},{2,1},{3,2},{4,3},{5,4},{6,5},{7,6},{8,15},{9,8},{10,9... | collective-permute-start | bytes 589832 | tf_op jit(solution)/shard_map/while/body/eval_jaxpr/ppermute | solution.py:16
  406.6 12.1 %collective-permute-start.5 = (bf16[128,768]{0,1:T(8,128)(2,1)S(1)}, bf16[128,768]{0,1:T(8,128)(2,1)S(1)}, u32[]{:S(2)}, u32[]{:S(2)}) collective-permute-start(bf16[128,768]{0,1:T(8,128)(2,1)S(1)} %add_convert_fusion), channel_id=1, source_target_pairs={{0,7},{1,0},{2,1},{3,2},{4,3},{5,4},{6,5},{7,6},{8,15},{9,8},{10,9... | collective-permute-start | bytes 589832 | tf_op jit(solution)/shard_map/ppermute | solution.py:16
  423.9 107.7 %reduce-scatter.9.cloned.1.call-start = ((), (), s32[]{:S(2)}) async-start(), calls=%async_computation.12 | async-start | bytes 5898240 | tf_op jit(solution)/shard_map/reduce_scatter | solution.py:249
  428.7 162.7 %reduce-scatter.11.cloned.1.call-start = ((), (), s32[]{:S(2)}) async-start(), calls=%async_computation.13 | async-start | bytes 5898240 | tf_op jit(solution)/shard_map/reduce_scatter | solution.py:252
  435.1 244.3 %all-reduce.4.cloned.1.call-start = ((), (), s32[]{:S(2)}) async-start(), calls=%async_computation.14 | async-start | bytes 7077888 | tf_op jit(solution)/shard_map/psum | solution.py:257
  (52 other events, 1142.0 us)
Sparse Core Ops, SparseCore 0:
  9.9 49.8 all-gather.6
  63.3 25.2 all-gather.8
  90.8 24.3 all-gather.10
  116.9 26.7 all-gather.12
  145.4 56.9 all-gather.14
  204.0 56.9 all-gather.16
  273.2 28.6 reduce-scatter.6
  424.0 47.5 reduce-scatter.4
  474.6 56.9 reduce-scatter.8
  534.4 56.9 reduce-scatter.10
  594.1 85.2 all-reduce.3
where the time goes:
time: 694 us; the launch traced here: 693 us
  waiting for transfers between devices  448 us (65%)
  starting transfers between devices  66.9 us (10%)
  local copies, waits for them, and re-layouts  51.3 us (7%)
  matrix products  45.4 us (7%)
  blocking collectives  42 us (6%)
  other arithmetic  22.7 us (3%)
  between operations  14.4 us (2%)
    ppermute x30, starting transfers between devices, from_behind(): return lax.ppermute(value, axis, pairs)  66.2 us
    reduce_scatter x1, waiting for transfers between devices, body(): lax.psum_scatter(local_mats[2].astype(jnp.bfloat16), 'dp', scatter_dimens...  60 us
    reduce_scatter x1, waiting for transfers between devices, body(): lax.psum_scatter(local_mats[3].astype(jnp.bfloat16), 'dp', scatter_dimens...  59.8 us
    all_gather x1, waiting for transfers between devices, body(): lax.all_gather(up_weight, 'dp', axis=0, tiled=True)  56.1 us
    all_gather x1, waiting for transfers between devices, body(): lax.all_gather(down_weight, 'dp', axis=0, tiled=True)  54.3 us
    all_gather x1, waiting for transfers between devices, body(): lax.all_gather(mix_weight, 'dp', axis=0, tiled=True)  49.4 us
    psum x1, blocking collectives, body(): lax.psum((first_gain_grad, first_shift_grad, query_bias_grad, value_bias_...  42 us
    ppermute x30, waiting for transfers between devices, from_behind(): return lax.ppermute(value, axis, pairs)  41.2 us
  transfers between devices with their start and end apart: 41, of which 26 were waited for; matrix products, arithmetic and copies ran while one was open for 13% of the time, Pallas kernels for 0%

commit v1 on v0

--- a/solution.py
+++ b/solution.py
@@ -3,6 +3,7 @@
 import jax.numpy as jnp
 from jax import lax
 from jax.sharding import PartitionSpec as P
+from jax.lax import all_gather
 
 H = 12
 HD = 64
@@ -69,6 +70,10 @@
     down_weight,
     down_bias,
 ):
+
+    def solve_rails_up(base_x):
+        return jnp.sum(all_gather(base_x, "ctx"), 0)
+
     rows = block_input.shape[1]
     width = block_input.shape[2]
     scale = HD ** (-0.5)
@@ -254,7 +259,7 @@
         ).astype(jnp.float32),
     )
     mats = (
-        lax.psum(shard_sums[0].astype(jnp.bfloat16), "ctx").astype(jnp.float32),
+        solve_rails_up(shard_sums[0].astype(jnp.bfloat16)).astype(jnp.float32),
         lax.psum(shard_sums[1].astype(jnp.bfloat16), "ctx").astype(jnp.float32),
         lax.psum(shard_sums[2].astype(jnp.bfloat16), "ctx").astype(jnp.float32),
         lax.psum(shard_sums[3].astype(jnp.bfloat16), "ctx").astype(jnp.float32),

time: 694 us -> 633 us (0.912)
  waiting for transfers between devices: 448 us -> 395 us
  local copies, waits for them, and re-layouts: 51.3 us -> 44.3 us
    all_gather x0 -> x1, waiting for transfers between devices: none -> 65.7 us  [solve_rails_up(): return jnp.sum(all_gather(base_x, 'ctx'), 0)]
    reduce_scatter x1, waiting for transfers between devices: 60 us -> 0.02 us  [body(): lax.psum_scatter(local_mats[2].astype(jnp.bfloat16), 'dp', scatter_dimens...]
    reduce_scatter x1, waiting for transfers between devices: 59.8 us -> 0.02 us  [body(): lax.psum_scatter(local_mats[3].astype(jnp.bfloat16), 'dp', scatter_dimens...]
    psum x1, waiting for transfers between devices: 37.8 us -> 23.7 us  [body(): lax.psum(shard_sums[1].astype(jnp.bfloat16), 'ctx').astype(jnp.float32)]
    reduce_scatter x1, waiting for transfers between devices: 36.4 us -> 47 us  [body(): lax.psum_scatter(local_mats[0].astype(jnp.bfloat16), 'dp', scatter_dimens...]
  transfers between devices with their start and end apart: 41 -> 42, of which waited for: 26 -> 25; matrix products, arithmetic and copies ran while one was open for 13% -> 15% of each run, Pallas kernels for 0% -> 0%
where the time goes in v1:
time: 633 us; the launch traced here: 632 us
  waiting for transfers between devices  395 us (62%)
  starting transfers between devices  62.8 us (10%)
  local copies, waits for them, and re-layouts  44.3 us (7%)
  matrix products  43 us (7%)
  blocking collectives  41.9 us (7%)
  other arithmetic  27.5 us (4%)
  between operations  14.9 us (2%)
    all_gather x1, waiting for transfers between devices, solve_rails_up(): return jnp.sum(all_gather(base_x, 'ctx'), 0)  65.7 us
    ppermute x30, starting transfers between devices, from_behind(): return lax.ppermute(value, axis, pairs)  62.2 us
    all_gather x1, waiting for transfers between devices, body(): lax.all_gather(up_weight, 'dp', axis=0, tiled=True)  55.9 us
    all_gather x1, waiting for transfers between devices, body(): lax.all_gather(down_weight, 'dp', axis=0, tiled=True)  55.3 us
    all_gather x1, waiting for transfers between devices, body(): lax.all_gather(mix_weight, 'dp', axis=0, tiled=True)  49.4 us
    reduce_scatter x1, waiting for transfers between devices, body(): lax.psum_scatter(local_mats[0].astype(jnp.bfloat16), 'dp', scatter_dimens...  47 us
    psum x1, blocking collectives, body(): lax.psum((first_gain_grad, first_shift_grad, query_bias_grad, value_bias_...  41.9 us
    ppermute x30, waiting for transfers between devices, from_behind(): return lax.ppermute(value, axis, pairs)  41.1 us
  transfers between devices with their start and end apart: 42, of which 25 were waited for; matrix products, arithmetic and copies ran while one was open for 15% of the time, Pallas kernels for 0%

profile of v1, /device:TPU:0, one launch (start us, length us, event | category | flops | bytes accessed | tf_op | source)
XLA Modules:
  0.0 631.7 jit_solution(4169378867823712913)
XLA Ops:
  10.4 49.4 %all-gather.9.cloned.1.call-done = bf16[768,2304]{1,0:T(8,128)(2,1)} async-done(((bf16[192,2304]{1,0:T(8,128)(2,1)}), bf16[768,2304]{1,0:T(8,128)(2,1)}) %all-gather.9.cloned.1.call-update) | async-done | bytes 3538960 | tf_op jit(solution)/shard_map/all_gather | solution.py:83
  66.0 22.6 %all-gather.11.cloned.1.call-done = bf16[1024,768]{1,0:T(8,128)(2,1)} async-done(((bf16[128,768]{1,0:T(8,128)(2,1)}), bf16[1024,768]{1,0:T(8,128)(2,1)}) %all-gather.11.cloned.1.call-update) | async-done | bytes 1572880 | tf_op jit(solution)/shard_map/all_gather | solution.py:105
  94.4 20.3 %all-gather.13.cloned.1.call-done = bf16[1024,768]{1,0:T(8,128)(2,1)} async-done(((bf16[128,768]{1,0:T(8,128)(2,1)}), bf16[1024,768]{1,0:T(8,128)(2,1)}) %all-gather.13.cloned.1.call-update) | async-done | bytes 1572880 | tf_op jit(solution)/shard_map/all_gather | solution.py:106
  117.3 3.8 reshape.243
  124.1 7.8 %while.39 = (s32[]{:T(128)}, f32[12,128]{1,0:T(8,128)S(1)}, f32[12,128]{1,0:T(8,128)S(1)}, f32[12,128,64]{1,2,0:T(8,128)S(1)}, s32[2]{0:T(128)S(1)}, /*index=5*/...) while((s32[]{:T(128)}, f32[12,128]{1,0:T(8,128)S(1)}, ...), condition=%wide.region_7.8_spmd.clone, body=%wide.region_2.7_spmd.clone.sunk | while | flops 714346112 | bytes 18655556 | solution.py:139
  125.3 5.2 conditional.8
  131.9 11.2 %all-gather.15.cloned.1.call-done = bf16[768,768]{1,0:T(8,128)(2,1)} async-done(((bf16[192,768]{1,0:T(8,128)(2,1)}), bf16[768,768]{1,0:T(8,128)(2,1)}) %all-gather.15.cloned.1.call-update) | async-done | bytes 1179664 | tf_op jit(solution)/shard_map/all_gather | solution.py:84
  145.9 55.9 %all-gather.17.cloned.1.call-done = bf16[768,3072]{1,0:T(8,128)(2,1)} async-done(((bf16[192,3072]{1,0:T(8,128)(2,1)}), bf16[768,3072]{1,0:T(8,128)(2,1)}) %all-gather.17.cloned.1.call-update) | async-done | bytes 4718608 | tf_op jit(solution)/shard_map/all_gather | solution.py:85
  205.1 55.3 %all-gather.19.cloned.1.call-done = bf16[3072,768]{1,0:T(8,128)(2,1)} async-done(((bf16[768,768]{1,0:T(8,128)(2,1)}), bf16[3072,768]{1,0:T(8,128)(2,1)}) %all-gather.19.cloned.1.call-update) | async-done | bytes 4718608 | tf_op jit(solution)/shard_map/all_gather | solution.py:86
  260.4 4.9 fusion.63
  270.3 4.9 convolution_convert_fusion.1
  275.3 3.7 convolution_convert_fusion
  284.9 124.9 %while.40 = (s32[]{:T(128)}, bf16[128,768]{0,1:T(8,128)(2,1)}, bf16[128,768]{0,1:T(8,128)(2,1)}, f32[128,768]{0,1:T(8,128)S(1)}, f32[128,768]{0,1:T(8,128)S(1)},...) while((s32[]{:T(128)}, bf16[128,768]{0,1:T(8,128)(2,1)}, ...), condition=%wide.region_16.17_spmd.clone, body=%wide.region_13.16_spmd.clone.sunk | while | flops 128401680 | bytes 14401084 | solution.py:229
  291.6 4.6 conditional.9
  304.1 3.7 collective-permute-start
  310.3 4.4 collective-permute-start.2
  322.0 3.7 collective-permute-start
  328.2 4.5 collective-permute-start.2
  339.9 3.7 collective-permute-start
  346.0 4.6 collective-permute-start.2
  357.8 3.7 collective-permute-start
  363.9 4.5 collective-permute-start.2
  375.6 3.7 collective-permute-start
  381.8 4.5 collective-permute-start.2
  399.7 4.5 collective-permute-start.2
  410.0 8.3 %collective-permute-start.5 = (bf16[128,768]{0,1:T(8,128)(2,1)S(1)}, bf16[128,768]{0,1:T(8,128)(2,1)S(1)}, u32[]{:S(2)}, u32[]{:S(2)}) collective-permute-start(bf16[128,768]{0,1:T(8,128)(2,1)S(1)} %add_convert_fusion), channel_id=1, source_target_pairs={{0,7},{1,0},{2,1},{3,2},{4,3},{5,4},{6,5},{7,6},{8,15},{9,8},{10,9... | collective-permute-start | bytes 589832 | tf_op jit(solution)/shard_map/ppermute | solution.py:17
  427.4 47.0 %reduce-scatter.5.cloned.1.call-done = bf16[192,2304]{1,0:T(8,128)(2,1)} async-done(((bf16[768,2304]{1,0:T(8,128)(2,1)}), bf16[192,2304]{1,0:T(8,128)(2,1)}) %reduce-scatter.5.cloned.1.call-update) | async-done | bytes 884752 | tf_op jit(solution)/shard_map/reduce_scatter | solution.py:248
  474.6 4.3 fusion.46
  480.5 41.9 %all-reduce = (f32[768]{0:T(1024)}, f32[768]{0:T(1024)}, f32[768]{0:T(1024)}, f32[768]{0:T(1024)}, f32[768]{0:T(1024)}, /*index=5*/f32[768]{0:T(1024)}, f32[768]{0:T(1024)}, f32[3072]{0:T(1024)}, f32[768]{0:T(1024)}) all-reduce(f32[768]{0:T(1024)S(1)} %get-tuple-element.662, ...), channel_id=1, replica_groups=mesh['dp'=4,'ctx'=8] {'dp','ctx'}, use_global_device_ids=true, to_apply=%region_22.23 | all-reduce | flops 9216 | bytes 73728 | tf_op jit(solution)/shard_map/psum | solution.py:267
  523.3 23.7 %all-reduce.4.cloned.1.call-done = (bf16[192,768]{1,0:T(8,128)(2,1)}, bf16[192,3072]{1,0:T(8,128)(2,1)}, bf16[768,768]{1,0:T(8,128)(2,1)}) async-done(((bf16[192,768]{1,0:T(8,128)(2,1)}, bf16[192,3072]{1,0:T(8,128)(2,1)}, bf16[768,768]{1,0:T(8,128)(2,1)}), (bf16[192,768]{1,0:T(8,128)(2,1)}, bf16[192,3072]{1,0:T(8,128)(2,1)}, bf16[768,768]{1,0:T(8,128)(2,1)})) %all-reduce.4.cloned.1.call-update) | async-done | bytes 2654224 | tf_op jit(solution)/shard_map/psum | solution.py:263
  553.4 65.7 %all-gather.21.cloned.1.call-done = bf16[1536,2304]{1,0:T(8,128)(2,1)} async-done(((bf16[192,2304]{1,0:T(8,128)(2,1)}), bf16[1536,2304]{1,0:T(8,128)(2,1)}) %all-gather.21.cloned.1.call-update) | async-done | bytes 7077904 | tf_op jit(solution)/shard_map/all_gather | solution.py:75
  619.1 4.4 reduce_sum.196
  (311 shorter events, 142.5 us)
Async XLA Ops:
  7.2 52.5 %all-gather.9.cloned.1.call-start = ((), (), s32[]{:S(2)}) async-start(), calls=%async_computation.4 | async-start | bytes 4423680 | tf_op jit(solution)/shard_map/all_gather | solution.py:83
  7.9 80.7 %all-gather.11.cloned.1.call-start = ((), (), s32[]{:S(2)}) async-start(), calls=%async_computation.5 | async-start | bytes 1769472 | tf_op jit(solution)/shard_map/all_gather | solution.py:105
  63.2 51.5 %all-gather.13.cloned.1.call-start = ((), (), s32[]{:S(2)}) async-start(), calls=%async_computation.6 | async-start | bytes 1769472 | tf_op jit(solution)/shard_map/all_gather | solution.py:106
  64.0 79.1 %all-gather.15.cloned.1.call-start = ((), (), s32[]{:S(2)}) async-start(), calls=%async_computation.7 | async-start | bytes 1474560 | tf_op jit(solution)/shard_map/all_gather | solution.py:84
  64.6 137.2 %all-gather.17.cloned.1.call-start = ((), (), s32[]{:S(2)}) async-start(), calls=%async_computation.8 | async-start | bytes 5898240 | tf_op jit(solution)/shard_map/all_gather | solution.py:85
  65.2 195.3 %all-gather.19.cloned.1.call-start = ((), (), s32[]{:S(2)}) async-start(), calls=%async_computation.9 | async-start | bytes 5898240 | tf_op jit(solution)/shard_map/all_gather | solution.py:86
  65.8 360.9 %reduce-scatter.7.cloned.1.call-start = ((), (), s32[]{:S(2)}) async-start(), calls=%async_computation.11 | async-start | bytes 1474560 | tf_op jit(solution)/shard_map/reduce_scatter | solution.py:251
  270.1 156.7 %reduce-scatter.9.cloned.1.call-start = ((), (), s32[]{:S(2)}) async-start(), calls=%async_computation.12 | async-start | bytes 5898240 | tf_op jit(solution)/shard_map/reduce_scatter | solution.py:254
  275.2 151.5 %reduce-scatter.11.cloned.1.call-start = ((), (), s32[]{:S(2)}) async-start(), calls=%async_computation.13 | async-start | bytes 5898240 | tf_op jit(solution)/shard_map/reduce_scatter | solution.py:257
  279.1 195.4 %reduce-scatter.5.cloned.1.call-start = ((), (), s32[]{:S(2)}) async-start(), calls=%async_computation.10 | async-start | bytes 4423680 | tf_op jit(solution)/shard_map/reduce_scatter | solution.py:248
  286.5 15.9 %collective-permute-start = (bf16[128,768]{0,1:T(8,128)(2,1)}, bf16[128,768]{0,1:T(8,128)(2,1)}, u32[]{:S(2)}, u32[]{:S(2)}) collective-permute-start(bf16[128,768]{0,1:T(8,128)(2,1)} %copy.82), channel_id=1, source_target_pairs={{0,7},{1,0},{2,1},{3,2},{4,3},{5,4},{6,5},{7,6},{8,15},{9,8},{10,9... | collective-permute-start | bytes 589832 | tf_op jit(solution)/shard_map/while/body/eval_jaxpr/ppermute | solution.py:17
  290.7 11.7 %collective-permute-start.1 = (bf16[128,768]{0,1:T(8,128)(2,1)}, bf16[128,768]{0,1:T(8,128)(2,1)}, u32[]{:S(2)}, u32[]{:S(2)}) collective-permute-start(bf16[128,768]{0,1:T(8,128)(2,1)} %copy.83), channel_id=1, source_target_pairs={{0,7},{1,0},{2,1},{3,2},{4,3},{5,4},{6,5},{7,6},{8,15},{9,8},{10,9... | collective-permute-start | bytes 589832 | tf_op jit(solution)/shard_map/while/body/eval_jaxpr/ppermute | solution.py:17
  304.1 16.2 %collective-permute-start = (bf16[128,768]{0,1:T(8,128)(2,1)}, bf16[128,768]{0,1:T(8,128)(2,1)}, u32[]{:S(2)}, u32[]{:S(2)}) collective-permute-start(bf16[128,768]{0,1:T(8,128)(2,1)} %copy.82), channel_id=1, source_target_pairs={{0,7},{1,0},{2,1},{3,2},{4,3},{5,4},{6,5},{7,6},{8,15},{9,8},{10,9... | collective-permute-start | bytes 589832 | tf_op jit(solution)/shard_map/while/body/eval_jaxpr/ppermute | solution.py:17
  309.5 10.8 %collective-permute-start.1 = (bf16[128,768]{0,1:T(8,128)(2,1)}, bf16[128,768]{0,1:T(8,128)(2,1)}, u32[]{:S(2)}, u32[]{:S(2)}) collective-permute-start(bf16[128,768]{0,1:T(8,128)(2,1)} %copy.83), channel_id=1, source_target_pairs={{0,7},{1,0},{2,1},{3,2},{4,3},{5,4},{6,5},{7,6},{8,15},{9,8},{10,9... | collective-permute-start | bytes 589832 | tf_op jit(solution)/shard_map/while/body/eval_jaxpr/ppermute | solution.py:17
  322.0 16.2 %collective-permute-start = (bf16[128,768]{0,1:T(8,128)(2,1)}, bf16[128,768]{0,1:T(8,128)(2,1)}, u32[]{:S(2)}, u32[]{:S(2)}) collective-permute-start(bf16[128,768]{0,1:T(8,128)(2,1)} %copy.82), channel_id=1, source_target_pairs={{0,7},{1,0},{2,1},{3,2},{4,3},{5,4},{6,5},{7,6},{8,15},{9,8},{10,9... | collective-permute-start | bytes 589832 | tf_op jit(solution)/shard_map/while/body/eval_jaxpr/ppermute | solution.py:17
  327.3 10.9 %collective-permute-start.1 = (bf16[128,768]{0,1:T(8,128)(2,1)}, bf16[128,768]{0,1:T(8,128)(2,1)}, u32[]{:S(2)}, u32[]{:S(2)}) collective-permute-start(bf16[128,768]{0,1:T(8,128)(2,1)} %copy.83), channel_id=1, source_target_pairs={{0,7},{1,0},{2,1},{3,2},{4,3},{5,4},{6,5},{7,6},{8,15},{9,8},{10,9... | collective-permute-start | bytes 589832 | tf_op jit(solution)/shard_map/while/body/eval_jaxpr/ppermute | solution.py:17
  328.2 8.0 %collective-permute-start.2 = (bf16[128,768]{0,1:T(8,128)(2,1)}, bf16[128,768]{0,1:T(8,128)(2,1)S(1)}, u32[]{:S(2)}, u32[]{:S(2)}) collective-permute-start(bf16[128,768]{0,1:T(8,128)(2,1)} %fusion.105), channel_id=1, source_target_pairs={{0,7},{1,0},{2,1},{3,2},{4,3},{5,4},{6,5},{7,6},{8,15},{9,8},{10,9... | collective-permute-start | bytes 589832 | tf_op jit(solution)/shard_map/while/body/eval_jaxpr/ppermute | solution.py:17
  339.9 16.3 %collective-permute-start = (bf16[128,768]{0,1:T(8,128)(2,1)}, bf16[128,768]{0,1:T(8,128)(2,1)}, u32[]{:S(2)}, u32[]{:S(2)}) collective-permute-start(bf16[128,768]{0,1:T(8,128)(2,1)} %copy.82), channel_id=1, source_target_pairs={{0,7},{1,0},{2,1},{3,2},{4,3},{5,4},{6,5},{7,6},{8,15},{9,8},{10,9... | collective-permute-start | bytes 589832 | tf_op jit(solution)/shard_map/while/body/eval_jaxpr/ppermute | solution.py:17
  345.2 11.0 %collective-permute-start.1 = (bf16[128,768]{0,1:T(8,128)(2,1)}, bf16[128,768]{0,1:T(8,128)(2,1)}, u32[]{:S(2)}, u32[]{:S(2)}) collective-permute-start(bf16[128,768]{0,1:T(8,128)(2,1)} %copy.83), channel_id=1, source_target_pairs={{0,7},{1,0},{2,1},{3,2},{4,3},{5,4},{6,5},{7,6},{8,15},{9,8},{10,9... | collective-permute-start | bytes 589832 | tf_op jit(solution)/shard_map/while/body/eval_jaxpr/ppermute | solution.py:17
  346.0 8.1 %collective-permute-start.2 = (bf16[128,768]{0,1:T(8,128)(2,1)}, bf16[128,768]{0,1:T(8,128)(2,1)S(1)}, u32[]{:S(2)}, u32[]{:S(2)}) collective-permute-start(bf16[128,768]{0,1:T(8,128)(2,1)} %fusion.105), channel_id=1, source_target_pairs={{0,7},{1,0},{2,1},{3,2},{4,3},{5,4},{6,5},{7,6},{8,15},{9,8},{10,9... | collective-permute-start | bytes 589832 | tf_op jit(solution)/shard_map/while/body/eval_jaxpr/ppermute | solution.py:17
  357.8 16.2 %collective-permute-start = (bf16[128,768]{0,1:T(8,128)(2,1)}, bf16[128,768]{0,1:T(8,128)(2,1)}, u32[]{:S(2)}, u32[]{:S(2)}) collective-permute-start(bf16[128,768]{0,1:T(8,128)(2,1)} %copy.82), channel_id=1, source_target_pairs={{0,7},{1,0},{2,1},{3,2},{4,3},{5,4},{6,5},{7,6},{8,15},{9,8},{10,9... | collective-permute-start | bytes 589832 | tf_op jit(solution)/shard_map/while/body/eval_jaxpr/ppermute | solution.py:17
  363.1 10.9 %collective-permute-start.1 = (bf16[128,768]{0,1:T(8,128)(2,1)}, bf16[128,768]{0,1:T(8,128)(2,1)}, u32[]{:S(2)}, u32[]{:S(2)}) collective-permute-start(bf16[128,768]{0,1:T(8,128)(2,1)} %copy.83), channel_id=1, source_target_pairs={{0,7},{1,0},{2,1},{3,2},{4,3},{5,4},{6,5},{7,6},{8,15},{9,8},{10,9... | collective-permute-start | bytes 589832 | tf_op jit(solution)/shard_map/while/body/eval_jaxpr/ppermute | solution.py:17
  363.9 8.0 %collective-permute-start.2 = (bf16[128,768]{0,1:T(8,128)(2,1)}, bf16[128,768]{0,1:T(8,128)(2,1)S(1)}, u32[]{:S(2)}, u32[]{:S(2)}) collective-permute-start(bf16[128,768]{0,1:T(8,128)(2,1)} %fusion.105), channel_id=1, source_target_pairs={{0,7},{1,0},{2,1},{3,2},{4,3},{5,4},{6,5},{7,6},{8,15},{9,8},{10,9... | collective-permute-start | bytes 589832 | tf_op jit(solution)/shard_map/while/body/eval_jaxpr/ppermute | solution.py:17
  375.6 16.3 %collective-permute-start = (bf16[128,768]{0,1:T(8,128)(2,1)}, bf16[128,768]{0,1:T(8,128)(2,1)}, u32[]{:S(2)}, u32[]{:S(2)}) collective-permute-start(bf16[128,768]{0,1:T(8,128)(2,1)} %copy.82), channel_id=1, source_target_pairs={{0,7},{1,0},{2,1},{3,2},{4,3},{5,4},{6,5},{7,6},{8,15},{9,8},{10,9... | collective-permute-start | bytes 589832 | tf_op jit(solution)/shard_map/while/body/eval_jaxpr/ppermute | solution.py:17
  381.0 10.9 %collective-permute-start.1 = (bf16[128,768]{0,1:T(8,128)(2,1)}, bf16[128,768]{0,1:T(8,128)(2,1)}, u32[]{:S(2)}, u32[]{:S(2)}) collective-permute-start(bf16[128,768]{0,1:T(8,128)(2,1)} %copy.83), channel_id=1, source_target_pairs={{0,7},{1,0},{2,1},{3,2},{4,3},{5,4},{6,5},{7,6},{8,15},{9,8},{10,9... | collective-permute-start | bytes 589832 | tf_op jit(solution)/shard_map/while/body/eval_jaxpr/ppermute | solution.py:17
  381.8 8.0 %collective-permute-start.2 = (bf16[128,768]{0,1:T(8,128)(2,1)}, bf16[128,768]{0,1:T(8,128)(2,1)S(1)}, u32[]{:S(2)}, u32[]{:S(2)}) collective-permute-start(bf16[128,768]{0,1:T(8,128)(2,1)} %fusion.105), channel_id=1, source_target_pairs={{0,7},{1,0},{2,1},{3,2},{4,3},{5,4},{6,5},{7,6},{8,15},{9,8},{10,9... | collective-permute-start | bytes 589832 | tf_op jit(solution)/shard_map/while/body/eval_jaxpr/ppermute | solution.py:17
  393.6 16.2 %collective-permute-start = (bf16[128,768]{0,1:T(8,128)(2,1)}, bf16[128,768]{0,1:T(8,128)(2,1)}, u32[]{:S(2)}, u32[]{:S(2)}) collective-permute-start(bf16[128,768]{0,1:T(8,128)(2,1)} %copy.82), channel_id=1, source_target_pairs={{0,7},{1,0},{2,1},{3,2},{4,3},{5,4},{6,5},{7,6},{8,15},{9,8},{10,9... | collective-permute-start | bytes 589832 | tf_op jit(solution)/shard_map/while/body/eval_jaxpr/ppermute | solution.py:17
  398.9 10.9 %collective-permute-start.1 = (bf16[128,768]{0,1:T(8,128)(2,1)}, bf16[128,768]{0,1:T(8,128)(2,1)}, u32[]{:S(2)}, u32[]{:S(2)}) collective-permute-start(bf16[128,768]{0,1:T(8,128)(2,1)} %copy.83), channel_id=1, source_target_pairs={{0,7},{1,0},{2,1},{3,2},{4,3},{5,4},{6,5},{7,6},{8,15},{9,8},{10,9... | collective-permute-start | bytes 589832 | tf_op jit(solution)/shard_map/while/body/eval_jaxpr/ppermute | solution.py:17
  399.7 8.0 %collective-permute-start.2 = (bf16[128,768]{0,1:T(8,128)(2,1)}, bf16[128,768]{0,1:T(8,128)(2,1)S(1)}, u32[]{:S(2)}, u32[]{:S(2)}) collective-permute-start(bf16[128,768]{0,1:T(8,128)(2,1)} %fusion.105), channel_id=1, source_target_pairs={{0,7},{1,0},{2,1},{3,2},{4,3},{5,4},{6,5},{7,6},{8,15},{9,8},{10,9... | collective-permute-start | bytes 589832 | tf_op jit(solution)/shard_map/while/body/eval_jaxpr/ppermute | solution.py:17
  410.0 11.4 %collective-permute-start.5 = (bf16[128,768]{0,1:T(8,128)(2,1)S(1)}, bf16[128,768]{0,1:T(8,128)(2,1)S(1)}, u32[]{:S(2)}, u32[]{:S(2)}) collective-permute-start(bf16[128,768]{0,1:T(8,128)(2,1)S(1)} %add_convert_fusion), channel_id=1, source_target_pairs={{0,7},{1,0},{2,1},{3,2},{4,3},{5,4},{6,5},{7,6},{8,15},{9,8},{10,9... | collective-permute-start | bytes 589832 | tf_op jit(solution)/shard_map/ppermute | solution.py:17
  426.6 120.4 %all-reduce.4.cloned.1.call-start = ((), (), s32[]{:S(2)}) async-start(), calls=%async_computation.15 | async-start | bytes 5308416 | tf_op jit(solution)/shard_map/psum | solution.py:263
  427.4 191.8 %all-gather.21.cloned.1.call-start = ((), (), s32[]{:S(2)}) async-start(), calls=%async_computation.14 | async-start | bytes 7962624 | tf_op jit(solution)/shard_map/all_gather | solution.py:75
  (50 other events, 1117.4 us)
Sparse Core Ops, SparseCore 0:
  9.9 49.8 all-gather.8
  63.3 25.2 all-gather.10
  90.2 24.3 all-gather.12
  116.4 26.7 all-gather.14
  144.8 56.9 all-gather.16
  203.5 56.9 all-gather.18
  270.2 28.6 reduce-scatter.6
  301.9 56.9 reduce-scatter.8
  361.9 56.9 reduce-scatter.10
  426.8 47.6 reduce-scatter.4
  477.0 69.9 all-reduce.3
  548.5 70.5 all-gather.20
